TPU v7x, 256 devices: a whole 4x4x8 slice. The times are simulated.
256 devices in a mesh: chain: 2 (over core), leaf: 16 (over y, x), head: 8 (over z).
Axes of the slice: x: 4, y: 4, z: 8, core: 2. Of those that a mesh axis runs over, the one named last changes fastest.
Arguments:
- query_in: bfloat16 [16384, 16, 128], P(('chain', 'leaf'), 'head'), may hold values from -6 to 6
- key_in: bfloat16 [16384, 16, 128], P(('chain', 'leaf'), 'head'), may hold values from -120 to 120
- value_in: bfloat16 [16384, 16, 128], P(('chain', 'leaf'), 'head'), may hold values from -6 to 6
- gate_in: bfloat16 [16384, 16, 128], P(('chain', 'leaf'), 'head'), may hold values from -6 to 6
- write_strength: float32 [16, 16384], P('head', ('chain', 'leaf')), as said below
- log_decay: float32 [16, 16384], P('head', ('chain', 'leaf')), as said below
- doc_resets: int32 [256], P(('chain', 'leaf')), may hold values from 0 to 1, as said below
- conv_weight: float32 [3, 4, 16, 128], P(None, None, 'head'), may hold values from -3 to 3
- output_norm_gain: float32 [128], replicated, may hold values from 0.25 to 1.75
- output_projection_weight: bfloat16 [2048, 4096], P(None, 'head'), may hold values from -0.125 to 0.125
Outputs:
- mixed: bfloat16 [16384, 4096], P(('chain', 'leaf'), 'head')
Inputs may be any that keep to these rules, and one draw needn't show every extreme that they name: `write_strength`: strictly positive. `log_decay`: strictly negative. `doc_resets`: at least one block of every draw starts a document.
All inputs are finite; a program needn't handle non-finite values.
Results may differ from a plain program's by a relative error of at most 0.0064.
Values may be sent and summed in bfloat16 or wider, within the bound.
A program may use at most 64 MiB of HBM per device.

v0:
```python
import jax
import jax.numpy as jnp
from jax import lax
from jax.sharding import PartitionSpec as P

BLOCK = 64
highest = lax.Precision.HIGHEST
epsilon = 1e-06
SEQ = ("chain", "leaf")


def mm(spec, a, b):
    return jnp.einsum(spec, a, b, precision=highest, preferred_element_type=jnp.float32)


def from_behind(value, axis, steps):
    count = lax.axis_size(axis)
    initial, last = (max(0, -steps), min(count, count - steps))
    return lax.ppermute(value, axis, [(source, source + steps) for source in range(initial, last)])


def unit_rows(matrix):
    return matrix / jnp.sqrt(jnp.sum(matrix * matrix, axis=-1, keepdims=True) + epsilon)


def causal_filter(signal, rim_rows, weights):
    kernel = weights.shape[0]
    length = signal.shape[0]
    padded = jnp.concatenate([rim_rows, signal], axis=0)
    running = weights[0] * padded[0:length]
    for offset in range(1, kernel):
        running = running + weights[offset] * padded[offset : offset + length]
    return jax.nn.silu(running)


def unit_lower_inverse(lower):
    size = lower.shape[-1]
    row = lax.broadcasted_iota(jnp.int32, (size, size), 0)
    col = lax.broadcasted_iota(jnp.int32, (size, size), 1)
    inverse = jnp.broadcast_to(jnp.eye(size, dtype=jnp.float32), lower.shape)
    span = 1
    while span < size:
        pick = (
            (row // (2 * span) == col // (2 * span))
            & (row // span % 2 == 1)
            & (col // span % 2 == 0)
        )
        coupling = jnp.where(pick, lower, 0.0)
        inverse = lax.optimization_barrier(inverse)
        inverse = inverse - mm(
            "...ij,...jk->...ik", mm("...ij,...jk->...ik", inverse, coupling), inverse
        )
        span *= 2
    return inverse


def on_device(
    query_in,
    key_in,
    value_in,
    gate_in,
    write_strength,
    log_decay,
    doc_resets,
    conv_weight,
    output_norm_gain,
    output_projection_weight,
):
    length, head_count, depth_k = query_in.shape
    value_width = value_in.shape[2]
    kernel = conv_weight.shape[1]
    tail_rows = jnp.stack(
        [
            query_in[length - kernel + 1 :],
            key_in[length - kernel + 1 :],
            value_in[length - kernel + 1 :],
        ]
    )
    rim_rows = from_behind(tail_rows, SEQ, 1)
    query_conv = causal_filter(query_in, rim_rows[0], conv_weight[0])
    key_conv = causal_filter(key_in, rim_rows[1], conv_weight[1])
    value_conv = causal_filter(value_in, rim_rows[2], conv_weight[2])
    query_unit = (unit_rows(query_conv) * depth_k ** (-0.5)).astype(jnp.bfloat16)
    key_unit = unit_rows(key_conv).astype(jnp.bfloat16)
    value_act = value_conv.astype(jnp.bfloat16)
    blocks = length // BLOCK
    query_blk = query_unit.reshape(blocks, BLOCK, head_count, depth_k)
    key_blk = key_unit.reshape(blocks, BLOCK, head_count, depth_k)
    value_blk = value_act.reshape(blocks, BLOCK, head_count, value_width)
    key_gram = jnp.einsum("nthe,nshe->nhts", key_blk, key_blk, preferred_element_type=jnp.float32)
    query_gram = jnp.einsum(
        "nthe,nshe->nhts", query_blk, key_blk, preferred_element_type=jnp.float32
    )
    strength = write_strength.reshape(head_count, blocks, BLOCK).transpose(1, 0, 2)
    decays = log_decay.reshape(head_count, blocks, BLOCK).transpose(1, 0, 2)
    row_index = lax.broadcasted_iota(jnp.int32, (BLOCK, BLOCK), 0)
    col_index = lax.broadcasted_iota(jnp.int32, (BLOCK, BLOCK), 1)
    strict_mask = row_index > col_index
    causal_mask = row_index >= col_index
    cumulative = jnp.cumsum(decays, axis=-1)
    spread_log = cumulative[..., :, None] - cumulative[..., None, :]
    fading = jnp.where(causal_mask, jnp.exp(jnp.where(causal_mask, spread_log, 0.0)), 0.0)
    growth = jnp.exp(cumulative)
    lower = jnp.where(strict_mask, strength[..., :, None] * fading * key_gram, 0.0)
    mixing = fading * query_gram
    query_float = jnp.transpose(query_blk, (0, 2, 1, 3)).astype(jnp.float32)
    key_float = jnp.transpose(key_blk, (0, 2, 1, 3)).astype(jnp.float32)
    value_float = jnp.transpose(value_blk, (0, 2, 1, 3)).astype(jnp.float32)
    targets = jnp.concatenate(
        [strength[..., None] * value_float, (strength * growth)[..., None] * key_float], axis=-1
    )
    solved = mm("nhts,nhsf->nhtf", unit_lower_inverse(lower), targets)
    local_values = solved[..., :value_width]
    write_keys = solved[..., value_width:]
    tail_fade = jnp.exp(cumulative[..., -1:] - cumulative)
    decayed_addresses = tail_fade[..., None] * key_float
    key_eye = jnp.eye(depth_k, dtype=jnp.float32)
    keep_mat = (1 - doc_resets).astype(jnp.float32)[:, None, None, None]
    transition = keep_mat * (
        growth[..., -1, None, None] * key_eye - mm("nhce,nhcf->nhef", decayed_addresses, write_keys)
    )
    addition = mm("nhce,nhcf->nhef", decayed_addresses, local_values)
    query_eff = keep_mat * (
        growth[..., None] * query_float - mm("nhts,nhse->nhte", mixing, write_keys)
    )
    own_output = mm("nhts,nhsf->nhtf", mixing, local_values)
    carry = jnp.concatenate(
        [
            jnp.broadcast_to(key_eye, (head_count, depth_k, depth_k)),
            jnp.zeros((head_count, depth_k, value_width), jnp.float32),
        ],
        axis=-1,
    )
    starts = []
    for n in range(blocks):
        starts.append(carry)
        carry = mm("hij,hjk->hik", transition[n], carry)
        carry = carry.at[..., depth_k:].add(addition[n])
    starts = jnp.stack(starts)
    reach = mm("nhtd,nhde->nhte", query_eff, starts)
    partial_out = own_output + reach[..., depth_k:]
    reach_map = reach[..., :depth_k]
    device_trans = carry[..., :depth_k]
    device_state = carry[..., depth_k:]
    place = lax.axis_index(SEQ)
    count = lax.axis_size(SEQ)
    trans, state = (device_trans, device_state)
    stride = 1
    while stride < count:
        got_trans, got_state = from_behind((trans, state), SEQ, stride)
        has = place >= stride
        state = state + mm("hij,hjk->hik", trans, got_state)
        if stride * 2 < count:
            trans = jnp.where(has, mm("hij,hjk->hik", trans, got_trans), trans)
        stride *= 2
    incoming = from_behind(state, SEQ, 1)
    core = partial_out + mm("nhte,hef->nhtf", reach_map, incoming)
    core = jnp.transpose(core, (0, 2, 1, 3)).reshape(length, head_count, value_width)
    scale_rms = jnp.sqrt(jnp.mean(core * core, axis=-1, keepdims=True) + epsilon)
    normed = (
        core / scale_rms * output_norm_gain * jax.nn.silu(gate_in.astype(jnp.float32))
    ).astype(jnp.bfloat16)
    shard_piece = lax.all_gather(normed, "head", axis=1, tiled=True)
    count = shard_piece.shape[1]
    flat_piece = shard_piece.reshape(shard_piece.shape[0], count * value_width)
    mixed = jnp.dot(flat_piece, output_projection_weight, preferred_element_type=jnp.float32)
    return mixed.astype(jnp.bfloat16)


def solution(mesh):
    return jax.shard_map(
        on_device,
        mesh=mesh,
        in_specs=(
            P(("chain", "leaf"), "head", None),
            P(("chain", "leaf"), "head", None),
            P(("chain", "leaf"), "head", None),
            P(("chain", "leaf"), "head", None),
            P("head", ("chain", "leaf")),
            P("head", ("chain", "leaf")),
            P(("chain", "leaf")),
            P(None, None, "head", None),
            P(),
            P(None, "head"),
        ),
        out_specs=P(("chain", "leaf"), "head"),
        check_vma=False,
    )
```

profile of v0, /device:TPU:2, one launch (start us, length us, event | category | flops | bytes accessed | tf_op | source)
XLA Modules:
  0.0 157.1 jit_solution(13814795067078425158)
XLA Ops:
  6.5 1.1 copy.162
  7.7 1.0 copy.161
  8.7 1.0 copy.160
  10.3 3.4 %collective-permute-start = (bf16[3,3,2,128]{3,1,2,0:T(4,128)(2,1)}, bf16[3,3,2,128]{3,1,2,0:T(4,128)(2,1)}, u32[]{:S(2)}, u32[]{:S(2)}) collective-permute-start(bf16[3,3,2,128]{3,1,2,0:T(4,128)(2,1)} %pad_maximum_fusion.3), channel_id=1, source_target_pairs={{0,8},{8,16},{16,24},{24,32},{32,40},{40,48},{48,56},{56,64},{64,7... | collective-permute-start | bytes 13832 | tf_op jit(solution)/shard_map/ppermute | solution.py:19
  14.5 1.5 slice_bitcast_fusion.33
  15.9 0.8 reshape.339
  16.7 0.8 reshape.342
  18.1 1.1 subtract_convert_fusion
  19.2 0.7 fusion.41
  20.6 0.8 fusion.122
  23.9 0.8 broadcast_in_dim.62
  27.5 1.4 multiply_reduce_fusion.1
  38.0 1.0 fusion.5
  39.0 2.2 %fusion.15 = f32[8,2,128,128]{3,2,1,0:T(8,128)S(1)} fusion(f32[8,2,64,256]{3,2,1,0:T(8,128)S(1)} %fusion.5, f32[8,2,64]{2,1,0:T(2,128)S(1)} %copy.181, bf16[8,64,2,128]{3,1,0,2:T(8,128)(2,1)S(1)} %bitcast.218), kind=kOutput, calls=%fused_computation.43 | convolution fusion | flops 201588736 | bytes 1843200 | tf_op jit(solution)/shard_map/nhce,nhcf->nhef/dot_general | solution.py:13
  41.3 2.0 %fusion = f32[8,2,128,128]{3,2,1,0:T(8,128)S(1)} fusion(f32[128,128]{1,0:T(8,128)S(1)} %copy-done.3, f32[8,2]{1,0:T(8,128)S(1)} %bitcast.226, f32[8]{0:T(128)S(1)} %copy-done.21, f32[8,2,64,256]{3,2,1,0:T(8,128)S(1)} %fusion.5, f32[8,2,64]{2,1,0:T(2,128)S(1)} %copy.181, bf16[8,64,2,128]{3,1,0,2:T(8,128)(2,1)S(1)} %bitcast.219), kind=kOutput, calls=%fused_computation.1 | convolution fusion | flops 202375168 | bytes 1913344 | tf_op jit(solution)/shard_map/nhce,nhcf->nhef/dot_general | solution.py:13
  46.6 3.1 %collective-permute-start.2 = (f32[2,128,128]{2,1,0:T(8,128)S(1)}, f32[2,128,128]{2,1,0:T(8,128)S(1)}, u32[]{:S(2)}, u32[]{:S(2)}) collective-permute-start(f32[2,128,128]{2,1,0:T(8,128)S(1)} %get-tuple-element.105), channel_id=1, source_target_pairs={{0,8},{8,16},{16,24},{24,32},{32,40},{40,48},{48,56},{56,64},{64,7... | collective-permute-start | bytes 393224 | tf_op jit(solution)/shard_map/ppermute | solution.py:19
  49.7 3.4 %collective-permute-start.1 = (f32[2,128,128]{2,1,0:T(8,128)S(1)}, f32[2,128,128]{2,1,0:T(8,128)S(1)}, u32[]{:S(2)}, u32[]{:S(2)}) collective-permute-start(f32[2,128,128]{2,1,0:T(8,128)S(1)} %get-tuple-element.106), channel_id=1, source_target_pairs={{0,8},{8,16},{16,24},{24,32},{32,40},{40,48},{48,56},{56,64},{64,7... | collective-permute-start | bytes 393224 | tf_op jit(solution)/shard_map/ppermute | solution.py:19
  55.0 1.3 fusion.140
  56.8 4.3 %collective-permute-start.3 = (f32[2,128,128]{2,1,0:T(8,128)S(1)}, f32[2,128,128]{2,1,0:T(8,128)S(1)}, u32[]{:S(2)}, u32[]{:S(2)}) collective-permute-start(f32[2,128,128]{2,1,0:T(8,128)S(1)} %convolution_add_fusion.5), channel_id=1, source_target_pairs={{0,16},{8,24},{16,32},{24,40},{32,48},{40,56},{48,64},{56,72},{64,... | collective-permute-start | bytes 393224 | tf_op jit(solution)/shard_map/ppermute | solution.py:19
  61.4 4.0 %collective-permute-start.4 = (f32[2,128,128]{2,1,0:T(8,128)S(1)}, f32[2,128,128]{2,1,0:T(8,128)S(1)}, u32[]{:S(2)}, u32[]{:S(2)}) collective-permute-start(f32[2,128,128]{2,1,0:T(8,128)S(1)} %convolution_select_fusion.3), channel_id=1, source_target_pairs={{0,16},{8,24},{16,32},{24,40},{32,48},{40,56},{48,64},{56,72},{64,... | collective-permute-start | bytes 393224 | tf_op jit(solution)/shard_map/ppermute | solution.py:19
  65.7 4.1 %collective-permute-start.5 = (f32[2,128,128]{2,1,0:T(8,128)S(1)}, f32[2,128,128]{2,1,0:T(8,128)S(1)}, u32[]{:S(2)}, u32[]{:S(2)}) collective-permute-start(f32[2,128,128]{2,1,0:T(8,128)S(1)} %convolution_add_fusion.4), channel_id=1, source_target_pairs={{0,32},{8,40},{16,48},{24,56},{32,64},{40,72},{48,80},{56,88},{64,... | collective-permute-start | bytes 393224 | tf_op jit(solution)/shard_map/ppermute | solution.py:19
  70.1 4.4 %collective-permute-start.6 = (f32[2,128,128]{2,1,0:T(8,128)S(1)}, f32[2,128,128]{2,1,0:T(8,128)S(1)}, u32[]{:S(2)}, u32[]{:S(2)}) collective-permute-start(f32[2,128,128]{2,1,0:T(8,128)S(1)} %convolution_select_fusion.2), channel_id=1, source_target_pairs={{0,32},{8,40},{16,48},{24,56},{32,64},{40,72},{48,80},{56,88},{64,... | collective-permute-start | bytes 393224 | tf_op jit(solution)/shard_map/ppermute | solution.py:19
  74.8 4.5 %collective-permute-start.7 = (f32[2,128,128]{2,1,0:T(8,128)S(1)}, f32[2,128,128]{2,1,0:T(8,128)S(1)}, u32[]{:S(2)}, u32[]{:S(2)}) collective-permute-start(f32[2,128,128]{2,1,0:T(8,128)S(1)} %convolution_add_fusion.3), channel_id=1, source_target_pairs={{0,64},{8,72},{16,80},{24,88},{32,96},{40,104},{48,112},{56,120},{... | collective-permute-start | bytes 393224 | tf_op jit(solution)/shard_map/ppermute | solution.py:19
  79.6 3.4 %collective-permute-start.8 = (f32[2,128,128]{2,1,0:T(8,128)S(1)}, f32[2,128,128]{2,1,0:T(8,128)S(1)}, u32[]{:S(2)}, u32[]{:S(2)}) collective-permute-start(f32[2,128,128]{2,1,0:T(8,128)S(1)} %convolution_select_fusion.1), channel_id=1, source_target_pairs={{0,64},{8,72},{16,80},{24,88},{32,96},{40,104},{48,112},{56,120},{... | collective-permute-start | bytes 393224 | tf_op jit(solution)/shard_map/ppermute | solution.py:19
  83.3 1.8 %collective-permute-start.9 = (f32[2,128,128]{2,1,0:T(8,128)S(1)}, f32[2,128,128]{2,1,0:T(8,128)S(1)}, u32[]{:S(2)}, u32[]{:S(2)}) collective-permute-start(f32[2,128,128]{2,1,0:T(8,128)S(1)} %convolution_add_fusion.2), channel_id=1, source_target_pairs={{0,128},{8,136},{16,144},{24,152},{32,160},{40,168},{48,176},{56,1... | collective-permute-start | bytes 393224 | tf_op jit(solution)/shard_map/ppermute | solution.py:19
  86.4 5.1 %collective-permute-start.10 = (f32[2,128,128]{2,1,0:T(8,128)S(1)}, f32[2,128,128]{2,1,0:T(8,128)S(1)}, u32[]{:S(2)}, u32[]{:S(2)}) collective-permute-start(f32[2,128,128]{2,1,0:T(8,128)S(1)} %convolution_add_fusion.1), channel_id=1, source_target_pairs={{0,8},{8,16},{16,24},{24,32},{32,40},{40,48},{48,56},{56,64},{64,7... | collective-permute-start | bytes 393224 | tf_op jit(solution)/shard_map/ppermute | solution.py:19
  92.2 3.1 %collective-permute-done.10 = f32[2,128,128]{2,1,0:T(8,128)S(1)} collective-permute-done((f32[2,128,128]{2,1,0:T(8,128)S(1)}, f32[2,128,128]{2,1,0:T(8,128)S(1)}, u32[]{:S(2)}, u32[]{:S(2)}) %collective-permute-start.10) | collective-permute-done | bytes 131104 | tf_op jit(solution)/shard_map/ppermute | solution.py:19
  95.2 0.8 multiply_reduce_fusion
  96.1 0.9 fusion.28
  97.1 45.5 %all-gather.2.cloned.1.call-done = bf16[512,16,128]{2,0,1:T(8,128)(2,1)} async-done(((bf16[512,2,128]{2,0,1:T(8,128)(2,1)}), bf16[512,16,128]{2,0,1:T(8,128)(2,1)}) %all-gather.2.cloned.1.call-update) | async-done | bytes 2097168 | tf_op jit(solution)/shard_map/all_gather | solution.py:163
  142.7 3.9 %copy.185 = bf16[512,16,128]{0,2,1:T(8,128)(2,1)} copy(bf16[512,16,128]{2,0,1:T(8,128)(2,1)} %all-gather.2.cloned.1.call-done) | data formatting | bytes 4194304 | tf_op jit(solution)/shard_map/all_gather | solution.py:163
  146.6 3.7 %convolution_convert_fusion = bf16[512,512]{1,0:T(8,128)(2,1)} fusion(bf16[512,2048]{0,1:T(8,128)(2,1)} %bitcast.215, bf16[2048,512]{1,0:T(8,128)(2,1)S(1)} %copy-done), kind=kOutput, calls=%fused_computation.2 | convolution fusion | flops 1074003968 | bytes 4718592 | tf_op jit(solution)/shard_map/dot_general | solution.py:166
  (144 shorter events, 25.6 us)
Async XLA Ops:
  6.5 140.1 %copy-start = (bf16[2048,512]{1,0:T(8,128)(2,1)S(1)}, bf16[2048,512]{1,0:T(8,128)(2,1)}, u32[]{:S(2)}) copy-start(bf16[2048,512]{1,0:T(8,128)(2,1)} %param.35) | copy-start | bytes 6291460
  6.5 136.1 %all-gather.2.cloned.1.call-start = ((), (), s32[]{:S(2)}) async-start(), calls=%async_computation | async-start | bytes 2359296 | tf_op jit(solution)/shard_map/all_gather | solution.py:163
  10.3 16.5 %collective-permute-start = (bf16[3,3,2,128]{3,1,2,0:T(4,128)(2,1)}, bf16[3,3,2,128]{3,1,2,0:T(4,128)(2,1)}, u32[]{:S(2)}, u32[]{:S(2)}) collective-permute-start(bf16[3,3,2,128]{3,1,2,0:T(4,128)(2,1)} %pad_maximum_fusion.3), channel_id=1, source_target_pairs={{0,8},{8,16},{16,24},{24,32},{32,40},{40,48},{48,56},{56,64},{64,7... | collective-permute-start | bytes 13832 | tf_op jit(solution)/shard_map/ppermute | solution.py:19
  14.4 8.9 %copy-start.2 = (f32[128,128]{1,0:T(8,128)}, f32[128,128]{1,0:T(8,128)S(1)}, u32[]{:S(2)}) copy-start(f32[128,128]{1,0:T(8,128)S(1)} %fusion.84) | copy-start | bytes 196612
  26.8 2.4 %copy-start.11 = (f32[8,2,64]{2,1,0:T(2,128)S(1)}, f32[8,2,64]{2,1,0:T(2,128)}, u32[]{:S(2)}) copy-start(f32[8,2,64]{2,1,0:T(2,128)} %copy.169) | copy-start | bytes 12292
  26.8 2.4 %copy-start.14 = (pred[64,64]{1,0:T(8,128)(4,1)S(1)}, pred[64,64]{1,0:T(8,128)(4,1)}, u32[]{:S(2)}) copy-start(pred[64,64]{1,0:T(8,128)(4,1)} %get-tuple-element.135) | copy-start | bytes 12292
  26.8 2.4 %copy-start.15 = (f32[8,2,64]{2,1,0:T(2,128)S(1)}, f32[8,2,64]{2,1,0:T(2,128)}, u32[]{:S(2)}) copy-start(f32[8,2,64]{2,1,0:T(2,128)} %copy.158) | copy-start | bytes 12292
  26.8 2.4 %copy-start.16 = (pred[64,64]{1,0:T(8,128)(4,1)S(1)}, pred[64,64]{1,0:T(8,128)(4,1)}, u32[]{:S(2)}) copy-start(pred[64,64]{1,0:T(8,128)(4,1)} %get-tuple-element.134) | copy-start | bytes 12292
  26.8 2.8 %copy-start.9 = (pred[64,64]{1,0:T(8,128)(4,1)S(1)}, pred[64,64]{1,0:T(8,128)(4,1)}, u32[]{:S(2)}) copy-start(pred[64,64]{1,0:T(8,128)(4,1)} %get-tuple-element.130) | copy-start | bytes 12292
  30.3 2.0 %copy-start.7 = (pred[64,64]{1,0:T(8,128)(4,1)S(1)}, pred[64,64]{1,0:T(8,128)(4,1)}, u32[]{:S(2)}) copy-start(pred[64,64]{1,0:T(8,128)(4,1)} %get-tuple-element.128) | copy-start | bytes 12292
  31.6 2.0 %copy-start.6 = (pred[64,64]{1,0:T(8,128)(4,1)S(1)}, pred[64,64]{1,0:T(8,128)(4,1)}, u32[]{:S(2)}) copy-start(pred[64,64]{1,0:T(8,128)(4,1)} %get-tuple-element.127) | copy-start | bytes 12292
  32.9 2.0 %copy-start.5 = (pred[64,64]{1,0:T(8,128)(4,1)S(1)}, pred[64,64]{1,0:T(8,128)(4,1)}, u32[]{:S(2)}) copy-start(pred[64,64]{1,0:T(8,128)(4,1)} %get-tuple-element.126) | copy-start | bytes 12292
  38.0 3.2 %copy-start.3 = (f32[128,128]{1,0:T(8,128)S(1)}, f32[128,128]{1,0:T(8,128)}, u32[]{:S(2)}) copy-start(f32[128,128]{1,0:T(8,128)} %copy-done.2) | copy-start | bytes 196612
  38.0 3.2 %copy-start.13 = (f32[8,2,1]{1,0,2:T(8,128)S(1)}, f32[8,2,1]{1,0,2:T(8,128)}, u32[]{:S(2)}) copy-start(f32[8,2,1]{1,0,2:T(8,128)} %copy.186) | copy-start | bytes 196
  38.0 3.2 %copy-start.21 = (f32[8]{0:T(128)S(1)}, f32[8]{0:T(128)}, u32[]{:S(2)}) copy-start(f32[8]{0:T(128)} %subtract_convert_fusion) | copy-start | bytes 100
  44.9 8.2 %copy-start.1 = (f32[8,2,128,256]{3,2,1,0:T(8,128)S(1)}, f32[8,2,128,256]{3,2,1,0:T(8,128)}, u32[]{:S(2)}) copy-start(f32[8,2,128,256]{3,2,1,0:T(8,128)} %fusion.41) | copy-start | bytes 6291460
  46.5 6.8 %copy-start.17 = (f32[2,128]{1,0:T(2,128)S(1)}, f32[2,128]{1,0:T(2,128)}, u32[]{:S(2)}) copy-start(f32[2,128]{1,0:T(2,128)} %get-tuple-element.113) | copy-start | bytes 3076
  46.5 6.8 %copy-start.18 = (f32[2,128]{1,0:T(2,128)S(1)}, f32[2,128]{1,0:T(2,128)}, u32[]{:S(2)}) copy-start(f32[2,128]{1,0:T(2,128)} %get-tuple-element.114) | copy-start | bytes 3076
  46.5 6.8 %copy-start.19 = (f32[2,128]{1,0:T(2,128)S(1)}, f32[2,128]{1,0:T(2,128)}, u32[]{:S(2)}) copy-start(f32[2,128]{1,0:T(2,128)} %get-tuple-element.115) | copy-start | bytes 3076
  46.5 6.8 %copy-start.20 = (f32[2,128]{1,0:T(2,128)S(1)}, f32[2,128]{1,0:T(2,128)}, u32[]{:S(2)}) copy-start(f32[2,128]{1,0:T(2,128)} %get-tuple-element.116) | copy-start | bytes 3076
  46.6 14.6 %collective-permute-start.2 = (f32[2,128,128]{2,1,0:T(8,128)S(1)}, f32[2,128,128]{2,1,0:T(8,128)S(1)}, u32[]{:S(2)}, u32[]{:S(2)}) collective-permute-start(f32[2,128,128]{2,1,0:T(8,128)S(1)} %get-tuple-element.105), channel_id=1, source_target_pairs={{0,8},{8,16},{16,24},{24,32},{32,40},{40,48},{48,56},{56,64},{64,7... | collective-permute-start | bytes 393224 | tf_op jit(solution)/shard_map/ppermute | solution.py:19
  49.7 6.9 %collective-permute-start.1 = (f32[2,128,128]{2,1,0:T(8,128)S(1)}, f32[2,128,128]{2,1,0:T(8,128)S(1)}, u32[]{:S(2)}, u32[]{:S(2)}) collective-permute-start(f32[2,128,128]{2,1,0:T(8,128)S(1)} %get-tuple-element.106), channel_id=1, source_target_pairs={{0,8},{8,16},{16,24},{24,32},{32,40},{40,48},{48,56},{56,64},{64,7... | collective-permute-start | bytes 393224 | tf_op jit(solution)/shard_map/ppermute | solution.py:19
  56.8 8.7 %collective-permute-start.3 = (f32[2,128,128]{2,1,0:T(8,128)S(1)}, f32[2,128,128]{2,1,0:T(8,128)S(1)}, u32[]{:S(2)}, u32[]{:S(2)}) collective-permute-start(f32[2,128,128]{2,1,0:T(8,128)S(1)} %convolution_add_fusion.5), channel_id=1, source_target_pairs={{0,16},{8,24},{16,32},{24,40},{32,48},{40,56},{48,64},{56,72},{64,... | collective-permute-start | bytes 393224 | tf_op jit(solution)/shard_map/ppermute | solution.py:19
  61.4 8.4 %collective-permute-start.4 = (f32[2,128,128]{2,1,0:T(8,128)S(1)}, f32[2,128,128]{2,1,0:T(8,128)S(1)}, u32[]{:S(2)}, u32[]{:S(2)}) collective-permute-start(f32[2,128,128]{2,1,0:T(8,128)S(1)} %convolution_select_fusion.3), channel_id=1, source_target_pairs={{0,16},{8,24},{16,32},{24,40},{32,48},{40,56},{48,64},{56,72},{64,... | collective-permute-start | bytes 393224 | tf_op jit(solution)/shard_map/ppermute | solution.py:19
  65.7 8.8 %collective-permute-start.5 = (f32[2,128,128]{2,1,0:T(8,128)S(1)}, f32[2,128,128]{2,1,0:T(8,128)S(1)}, u32[]{:S(2)}, u32[]{:S(2)}) collective-permute-start(f32[2,128,128]{2,1,0:T(8,128)S(1)} %convolution_add_fusion.4), channel_id=1, source_target_pairs={{0,32},{8,40},{16,48},{24,56},{32,64},{40,72},{48,80},{56,88},{64,... | collective-permute-start | bytes 393224 | tf_op jit(solution)/shard_map/ppermute | solution.py:19
  70.1 9.2 %collective-permute-start.6 = (f32[2,128,128]{2,1,0:T(8,128)S(1)}, f32[2,128,128]{2,1,0:T(8,128)S(1)}, u32[]{:S(2)}, u32[]{:S(2)}) collective-permute-start(f32[2,128,128]{2,1,0:T(8,128)S(1)} %convolution_select_fusion.2), channel_id=1, source_target_pairs={{0,32},{8,40},{16,48},{24,56},{32,64},{40,72},{48,80},{56,88},{64,... | collective-permute-start | bytes 393224 | tf_op jit(solution)/shard_map/ppermute | solution.py:19
  74.8 8.2 %collective-permute-start.7 = (f32[2,128,128]{2,1,0:T(8,128)S(1)}, f32[2,128,128]{2,1,0:T(8,128)S(1)}, u32[]{:S(2)}, u32[]{:S(2)}) collective-permute-start(f32[2,128,128]{2,1,0:T(8,128)S(1)} %convolution_add_fusion.3), channel_id=1, source_target_pairs={{0,64},{8,72},{16,80},{24,88},{32,96},{40,104},{48,112},{56,120},{... | collective-permute-start | bytes 393224 | tf_op jit(solution)/shard_map/ppermute | solution.py:19
  79.6 5.9 %collective-permute-start.8 = (f32[2,128,128]{2,1,0:T(8,128)S(1)}, f32[2,128,128]{2,1,0:T(8,128)S(1)}, u32[]{:S(2)}, u32[]{:S(2)}) collective-permute-start(f32[2,128,128]{2,1,0:T(8,128)S(1)} %convolution_select_fusion.1), channel_id=1, source_target_pairs={{0,64},{8,72},{16,80},{24,88},{32,96},{40,104},{48,112},{56,120},{... | collective-permute-start | bytes 393224 | tf_op jit(solution)/shard_map/ppermute | solution.py:19
  83.3 2.8 %collective-permute-start.9 = (f32[2,128,128]{2,1,0:T(8,128)S(1)}, f32[2,128,128]{2,1,0:T(8,128)S(1)}, u32[]{:S(2)}, u32[]{:S(2)}) collective-permute-start(f32[2,128,128]{2,1,0:T(8,128)S(1)} %convolution_add_fusion.2), channel_id=1, source_target_pairs={{0,128},{8,136},{16,144},{24,152},{32,160},{40,168},{48,176},{56,1... | collective-permute-start | bytes 393224 | tf_op jit(solution)/shard_map/ppermute | solution.py:19
  86.4 9.8 %copy-start.4 = (bf16[512,2,128]{2,1,0:T(2,128)(2,1)S(1)}, bf16[512,2,128]{2,1,0:T(2,128)(2,1)}, u32[]{:S(2)}) copy-start(bf16[512,2,128]{2,1,0:T(2,128)(2,1)} %param.29) | copy-start | bytes 786436
  86.4 9.8 %copy-start.22 = (f32[128]{0:T(128)S(1)}, f32[128]{0:T(128)}, u32[]{:S(2)}) copy-start(f32[128]{0:T(128)} %param.34) | copy-start | bytes 1540
  86.4 8.8 %collective-permute-start.10 = (f32[2,128,128]{2,1,0:T(8,128)S(1)}, f32[2,128,128]{2,1,0:T(8,128)S(1)}, u32[]{:S(2)}, u32[]{:S(2)}) collective-permute-start(f32[2,128,128]{2,1,0:T(8,128)S(1)} %convolution_add_fusion.1), channel_id=1, source_target_pairs={{0,8},{8,16},{16,24},{24,32},{32,40},{40,48},{48,56},{56,64},{64,7... | collective-permute-start | bytes 393224 | tf_op jit(solution)/shard_map/ppermute | solution.py:19
  (3 other events, 4.8 us)
Sparse Core Ops, SparseCore 0:
  97.2 45.3 all-gather.1
where the time goes:
time: 158 us; the launch traced here: 157 us
  waiting for transfers between devices  49.5 us (31%)
  starting transfers between devices  41.6 us (26%)
  matrix products  26 us (16%)
  local copies, waits for them, and re-layouts  16.7 us (11%)
  between operations  14.4 us (9%)
  other arithmetic  8.9 us (6%)
    all_gather x1, waiting for transfers between devices, on_device(): shard_piece = lax.all_gather(normed, 'head', axis=1, tiled=True)  45.5 us
    ppermute x11, starting transfers between devices, from_behind(): lax.ppermute(value, axis, [(source, source + steps) for source in range(i...  41.6 us
    dot_general x36, matrix products, mm(): jnp.einsum(spec, a, b, precision=highest, preferred_element_type=jnp.floa...  21.7 us
    unnamed x56, local copies, waits for them, and re-layouts  4.06 us
    ppermute x11, waiting for transfers between devices, from_behind(): lax.ppermute(value, axis, [(source, source + steps) for source in range(i...  3.97 us
    all_gather x1, local copies, waits for them, and re-layouts, on_device(): shard_piece = lax.all_gather(normed, 'head', axis=1, tiled=True)  3.93 us
    dot_general x1, matrix products, on_device(): jnp.dot(flat_piece, output_projection_weight, preferred_element_type=jnp....  3.65 us
  transfers between devices with their start and end apart: 12, of which 5 were waited for; matrix products, arithmetic and copies ran while one was open for 12% of the time, Pallas kernels for 0%

commit v1 on v0

--- a/solution.py
+++ b/solution.py
@@ -7,6 +7,28 @@
 highest = lax.Precision.HIGHEST
 epsilon = 1e-06
 SEQ = ("chain", "leaf")
+
+
+def laid_out(blocks, dim):
+    blocks = jnp.moveaxis(blocks, 0, dim)
+    shape = blocks.shape
+    return blocks.reshape(*shape[:dim], shape[dim] * shape[dim + 1], *shape[dim + 2 :])
+
+
+def gather_around(x, axis, dim):
+    devices = lax.axis_size(axis)
+    pairs = [(i, (i + 1) % devices) for i in range(devices)]
+    back = [(b, a) for a, b in pairs]
+    lower, upper = ([], [])
+    for hop in range(devices - 1):
+        if hop % 2 == 0:
+            lower.append(lax.ppermute(lower[-1] if lower else x, axis, pairs))
+        else:
+            upper.append(lax.ppermute(upper[-1] if upper else x, axis, back))
+    parts = jnp.stack([*lower[::-1], x, *upper])
+    shift = lax.axis_index(axis) - len(lower)
+    parts = parts[(jnp.arange(devices) - shift) % devices]
+    return laid_out(parts, dim)
 
 
 def mm(spec, a, b):
@@ -160,7 +182,7 @@
     normed = (
         core / scale_rms * output_norm_gain * jax.nn.silu(gate_in.astype(jnp.float32))
     ).astype(jnp.bfloat16)
-    shard_piece = lax.all_gather(normed, "head", axis=1, tiled=True)
+    shard_piece = gather_around(normed, "head", 1)
     count = shard_piece.shape[1]
     flat_piece = shard_piece.reshape(shard_piece.shape[0], count * value_width)
     mixed = jnp.dot(flat_piece, output_projection_weight, preferred_element_type=jnp.float32)

time: 158 us -> 152 us (0.962); the launches traced: 157 us -> 149 us
  waiting for transfers between devices: 49.5 us -> 29.8 us
  between operations: 14.4 us -> 1.07 us
  local copies, waits for them, and re-layouts: 16.7 us -> 28.5 us
  starting transfers between devices: 41.6 us -> 53.4 us
    all_gather x1 -> x0, waiting for transfers between devices: 45.5 us -> none  [on_device(): shard_piece = lax.all_gather(normed, 'head', axis=1, tiled=True)]
    ppermute x0 -> x7, waiting for transfers between devices: none -> 25.9 us  [the longest x4 25.8 us: gather_around(): lower.append(lax.ppermute(lower[-1] if lower else x, axis, pairs))]
    ppermute x0 -> x7, starting transfers between devices: none -> 11.8 us  [the longest x3 9.78 us: gather_around(): upper.append(lax.ppermute(upper[-1] if upper else x, axis, back))]
    unnamed x56 -> x69, local copies, waits for them, and re-layouts: 4.06 us -> 11.3 us
    all_gather x1 -> x0, local copies, waits for them, and re-layouts: 3.93 us -> none  [on_device(): shard_piece = lax.all_gather(normed, 'head', axis=1, tiled=True)]
    transpose x0 -> x1, local copies, waits for them, and re-layouts: none -> 3.92 us  [laid_out(): blocks = jnp.moveaxis(blocks, 0, dim)]
    gather x0 -> x1, local copies, waits for them, and re-layouts: none -> 3.75 us  [gather_around(): parts = parts[(jnp.arange(devices) - shift) % devices]]
  transfers between devices with their start and end apart: 12 -> 18, of which waited for: 5 -> 8; matrix products, arithmetic and copies ran while one was open for 12% -> 17% of each run, Pallas kernels for 0% -> 0%
where the time goes in v1:
time: 152 us; the launch traced here: 149 us
  starting transfers between devices  53.4 us (35%)
  waiting for transfers between devices  29.8 us (20%)
  local copies, waits for them, and re-layouts  28.5 us (19%)
  matrix products  27.1 us (18%)
  other arithmetic  9.51 us (6%)
    ppermute x11, starting transfers between devices, from_behind(): lax.ppermute(value, axis, [(source, source + steps) for source in range(i...  41.6 us
    ppermute x4, waiting for transfers between devices, gather_around(): lower.append(lax.ppermute(lower[-1] if lower else x, axis, pairs))  25.8 us
    dot_general x36, matrix products, mm(): jnp.einsum(spec, a, b, precision=highest, preferred_element_type=jnp.floa...  22.8 us
    unnamed x69, local copies, waits for them, and re-layouts  11.3 us
    ppermute x3, starting transfers between devices, gather_around(): upper.append(lax.ppermute(upper[-1] if upper else x, axis, back))  9.78 us
    ppermute x11, waiting for transfers between devices, from_behind(): lax.ppermute(value, axis, [(source, source + steps) for source in range(i...  3.95 us
    transpose x1, local copies, waits for them, and re-layouts, laid_out(): blocks = jnp.moveaxis(blocks, 0, dim)  3.92 us
    gather x1, local copies, waits for them, and re-layouts, gather_around(): parts = parts[(jnp.arange(devices) - shift) % devices]  3.75 us
  transfers between devices with their start and end apart: 18, of which 8 were waited for; matrix products, arithmetic and copies ran while one was open for 17% of the time, Pallas kernels for 0%

profile of v1, /device:TPU:2, one launch (start us, length us, event | category | flops | bytes accessed | tf_op | source)
XLA Modules:
  0.0 149.3 jit_solution(15886612648421905361)
XLA Ops:
  4.0 3.4 %collective-permute-start = (bf16[3,3,2,128]{3,1,2,0:T(4,128)(2,1)}, bf16[3,3,2,128]{3,1,2,0:T(4,128)(2,1)}, u32[]{:S(2)}, u32[]{:S(2)}) collective-permute-start(bf16[3,3,2,128]{3,1,2,0:T(4,128)(2,1)} %pad_maximum_fusion.3), channel_id=1, source_target_pairs={{0,8},{8,16},{16,24},{24,32},{32,40},{40,48},{48,56},{56,64},{64,7... | collective-permute-start | bytes 13832 | tf_op jit(solution)/shard_map/ppermute | solution.py:41
  8.1 1.5 %slice_bitcast_fusion.33 = (f32[2,128]{1,0:T(2,128)}, f32[2,128]{1,0:T(2,128)}, f32[2,128]{1,0:T(2,128)}, f32[2,128]{1,0:T(2,128)}, f32[2,128]{1,0:T(2,128)}, /*...) fusion(f32[3,4,2,128]{3,2,1,0:T(2,128)} %param.33), kind=kLoop, calls=%fused_computation.298 | loop fusion | bytes 24576 | tf_op jit(solution)/shard_map/mul | solution.py:52
  11.7 1.2 subtract_convert_fusion
  21.4 2.6 %multiply_reduce_fusion.1 = (f32[512,2]{0,1:T(2,128)S(1)}, f32[512,2,128]{2,0,1:T(8,128)S(1)}, bf16[512,2,128]{2,0,1:T(8,128)(2,1)S(1)}) fusion(bf16[512,2,128]{2,0,1:T(8,128)(2,1)} %copy-done.4, f32[2,128]{1,0:T(2,128)} %get-tuple-element.109, bf16[3,2,128]{2,0,1:T(4,128)(2,1)S(1)} %get-tuple-element.123, f32[2,128]{1,0:T(2,128)} %get-tuple-element.110, ...), kind=kLoop, calls=%fused_computation.61 | loop fusion | flops 6683648 | bytes 1326080 | tf_op jit(solution)/shard_map/reduce_sum | solution.py:45
  25.3 1.8 %convolution_subtract_fusion.6 = f32[8,2,64,64]{3,2,1,0:T(8,128)S(1)} fusion(f32[8,2,64,64]{3,2,1,0:T(8,128)} %copy-done.1, f32[8,2,64,64]{3,2,1,0:T(8,128)S(1)} %fusion.26), kind=kOutput, calls=%fused_computation.9 | convolution fusion | flops 50397184 | bytes 786432 | tf_op jit(solution)/shard_map/...ij,...jk->...ik/dot_general | solution.py:35
  35.3 2.2 %fusion.15 = f32[8,2,128,128]{3,2,1,0:T(8,128)S(1)} fusion(f32[8,2,64,256]{3,2,1,0:T(8,128)S(1)} %fusion.5, f32[8,2,64]{2,1,0:T(2,128)S(1)} %copy.128, bf16[8,64,2,128]{3,1,0,2:T(8,128)(2,1)S(1)} %bitcast.238), kind=kOutput, calls=%fused_computation.44 | convolution fusion | flops 201588736 | bytes 1843200 | tf_op jit(solution)/shard_map/nhce,nhcf->nhef/dot_general | solution.py:35
  37.5 2.0 %fusion = f32[8,2,128,128]{3,2,1,0:T(8,128)S(1)} fusion(f32[128,128]{1,0:T(8,128)S(1)} %copy-done.6, f32[8,2]{1,0:T(8,128)S(1)} %bitcast.246, f32[8]{0:T(128)S(1)} %copy-done.24, f32[8,2,64,256]{3,2,1,0:T(8,128)S(1)} %fusion.5, f32[8,2,64]{2,1,0:T(2,128)S(1)} %copy.128, bf16[8,64,2,128]{3,1,0,2:T(8,128)(2,1)S(1)} %bitcast.239), kind=kOutput, calls=%fused_computation.2 | convolution fusion | flops 202375168 | bytes 1913344 | tf_op jit(solution)/shard_map/nhce,nhcf->nhef/dot_general | solution.py:35
  42.7 3.1 %collective-permute-start.2 = (f32[2,128,128]{2,1,0:T(8,128)S(1)}, f32[2,128,128]{2,1,0:T(8,128)S(1)}, u32[]{:S(2)}, u32[]{:S(2)}) collective-permute-start(f32[2,128,128]{2,1,0:T(8,128)S(1)} %get-tuple-element.105), channel_id=1, source_target_pairs={{0,8},{8,16},{16,24},{24,32},{32,40},{40,48},{48,56},{56,64},{64,7... | collective-permute-start | bytes 393224 | tf_op jit(solution)/shard_map/ppermute | solution.py:41
  45.9 3.4 %collective-permute-start.1 = (f32[2,128,128]{2,1,0:T(8,128)S(1)}, f32[2,128,128]{2,1,0:T(8,128)S(1)}, u32[]{:S(2)}, u32[]{:S(2)}) collective-permute-start(f32[2,128,128]{2,1,0:T(8,128)S(1)} %get-tuple-element.106), channel_id=1, source_target_pairs={{0,8},{8,16},{16,24},{24,32},{32,40},{40,48},{48,56},{56,64},{64,7... | collective-permute-start | bytes 393224 | tf_op jit(solution)/shard_map/ppermute | solution.py:41
  51.2 1.3 fusion.142
  53.0 4.3 %collective-permute-start.3 = (f32[2,128,128]{2,1,0:T(8,128)S(1)}, f32[2,128,128]{2,1,0:T(8,128)S(1)}, u32[]{:S(2)}, u32[]{:S(2)}) collective-permute-start(f32[2,128,128]{2,1,0:T(8,128)S(1)} %convolution_add_fusion.5), channel_id=1, source_target_pairs={{0,16},{8,24},{16,32},{24,40},{32,48},{40,56},{48,64},{56,72},{64,... | collective-permute-start | bytes 393224 | tf_op jit(solution)/shard_map/ppermute | solution.py:41
  57.6 4.0 %collective-permute-start.4 = (f32[2,128,128]{2,1,0:T(8,128)S(1)}, f32[2,128,128]{2,1,0:T(8,128)S(1)}, u32[]{:S(2)}, u32[]{:S(2)}) collective-permute-start(f32[2,128,128]{2,1,0:T(8,128)S(1)} %convolution_select_fusion.3), channel_id=1, source_target_pairs={{0,16},{8,24},{16,32},{24,40},{32,48},{40,56},{48,64},{56,72},{64,... | collective-permute-start | bytes 393224 | tf_op jit(solution)/shard_map/ppermute | solution.py:41
  61.9 4.1 %collective-permute-start.5 = (f32[2,128,128]{2,1,0:T(8,128)S(1)}, f32[2,128,128]{2,1,0:T(8,128)S(1)}, u32[]{:S(2)}, u32[]{:S(2)}) collective-permute-start(f32[2,128,128]{2,1,0:T(8,128)S(1)} %convolution_add_fusion.4), channel_id=1, source_target_pairs={{0,32},{8,40},{16,48},{24,56},{32,64},{40,72},{48,80},{56,88},{64,... | collective-permute-start | bytes 393224 | tf_op jit(solution)/shard_map/ppermute | solution.py:41
  66.3 4.4 %collective-permute-start.6 = (f32[2,128,128]{2,1,0:T(8,128)S(1)}, f32[2,128,128]{2,1,0:T(8,128)S(1)}, u32[]{:S(2)}, u32[]{:S(2)}) collective-permute-start(f32[2,128,128]{2,1,0:T(8,128)S(1)} %convolution_select_fusion.2), channel_id=1, source_target_pairs={{0,32},{8,40},{16,48},{24,56},{32,64},{40,72},{48,80},{56,88},{64,... | collective-permute-start | bytes 393224 | tf_op jit(solution)/shard_map/ppermute | solution.py:41
  71.1 4.5 %collective-permute-start.7 = (f32[2,128,128]{2,1,0:T(8,128)S(1)}, f32[2,128,128]{2,1,0:T(8,128)S(1)}, u32[]{:S(2)}, u32[]{:S(2)}) collective-permute-start(f32[2,128,128]{2,1,0:T(8,128)S(1)} %convolution_add_fusion.3), channel_id=1, source_target_pairs={{0,64},{8,72},{16,80},{24,88},{32,96},{40,104},{48,112},{56,120},{... | collective-permute-start | bytes 393224 | tf_op jit(solution)/shard_map/ppermute | solution.py:41
  75.8 3.4 %collective-permute-start.8 = (f32[2,128,128]{2,1,0:T(8,128)S(1)}, f32[2,128,128]{2,1,0:T(8,128)S(1)}, u32[]{:S(2)}, u32[]{:S(2)}) collective-permute-start(f32[2,128,128]{2,1,0:T(8,128)S(1)} %convolution_select_fusion.1), channel_id=1, source_target_pairs={{0,64},{8,72},{16,80},{24,88},{32,96},{40,104},{48,112},{56,120},{... | collective-permute-start | bytes 393224 | tf_op jit(solution)/shard_map/ppermute | solution.py:41
  79.5 1.8 %collective-permute-start.9 = (f32[2,128,128]{2,1,0:T(8,128)S(1)}, f32[2,128,128]{2,1,0:T(8,128)S(1)}, u32[]{:S(2)}, u32[]{:S(2)}) collective-permute-start(f32[2,128,128]{2,1,0:T(8,128)S(1)} %convolution_add_fusion.2), channel_id=1, source_target_pairs={{0,128},{8,136},{16,144},{24,152},{32,160},{40,168},{48,176},{56,1... | collective-permute-start | bytes 393224 | tf_op jit(solution)/shard_map/ppermute | solution.py:41
  82.6 5.1 %collective-permute-start.10 = (f32[2,128,128]{2,1,0:T(8,128)S(1)}, f32[2,128,128]{2,1,0:T(8,128)S(1)}, u32[]{:S(2)}, u32[]{:S(2)}) collective-permute-start(f32[2,128,128]{2,1,0:T(8,128)S(1)} %convolution_add_fusion.1), channel_id=1, source_target_pairs={{0,8},{8,16},{16,24},{24,32},{32,40},{40,48},{48,56},{56,64},{64,7... | collective-permute-start | bytes 393224 | tf_op jit(solution)/shard_map/ppermute | solution.py:41
  88.4 3.0 %collective-permute-done.10 = f32[2,128,128]{2,1,0:T(8,128)S(1)} collective-permute-done((f32[2,128,128]{2,1,0:T(8,128)S(1)}, f32[2,128,128]{2,1,0:T(8,128)S(1)}, u32[]{:S(2)}, u32[]{:S(2)}) %collective-permute-start.10) | collective-permute-done | bytes 131104 | tf_op jit(solution)/shard_map/ppermute | solution.py:41
  92.6 2.0 %collective-permute-start.11 = (bf16[512,2,128]{2,0,1:T(8,128)(2,1)S(1)}, bf16[512,2,128]{2,0,1:T(8,128)(2,1)S(1)}, u32[]{:S(2)}, u32[]{:S(2)}) collective-permute-start(bf16[512,2,128]{2,0,1:T(8,128)(2,1)S(1)} %fusion.28), channel_id=1, source_target_pairs={{0,1},{1,2},{2,3},{3,4},{4,5},{5,6},{6,7},{7,0},{8,9},{9,10},{10,1... | collective-permute-start | bytes 786440 | tf_op jit(solution)/shard_map/ppermute | solution.py:25
  94.6 10.5 %collective-permute-done.11 = bf16[512,2,128]{2,0,1:T(8,128)(2,1)S(1)} collective-permute-done((bf16[512,2,128]{2,0,1:T(8,128)(2,1)S(1)}, bf16[512,2,128]{2,0,1:T(8,128)(2,1)S(1)}, u32[]{:S(2)}, u32[]{:S(2)}) %collective-permute-start.11) | collective-permute-done | bytes 262176 | tf_op jit(solution)/shard_map/ppermute | solution.py:25
  105.1 3.2 %collective-permute-start.15 = (bf16[512,2,128]{2,0,1:T(8,128)(2,1)S(1)}, bf16[512,2,128]{2,0,1:T(8,128)(2,1)S(1)}, u32[]{:S(2)}, u32[]{:S(2)}) collective-permute-start(bf16[512,2,128]{2,0,1:T(8,128)(2,1)S(1)} %fusion.28), channel_id=1, source_target_pairs={{1,0},{2,1},{3,2},{4,3},{5,4},{6,5},{7,6},{0,7},{9,8},{10,9},{11,1... | collective-permute-start | bytes 786440 | tf_op jit(solution)/shard_map/ppermute | solution.py:27
  108.3 5.8 %collective-permute-done.12 = bf16[512,2,128]{2,0,1:T(8,128)(2,1)S(1)} collective-permute-done((bf16[512,2,128]{2,0,1:T(8,128)(2,1)S(1)}, bf16[512,2,128]{2,0,1:T(8,128)(2,1)S(1)}, u32[]{:S(2)}, u32[]{:S(2)}) %collective-permute-start.12) | collective-permute-done | bytes 262176 | tf_op jit(solution)/shard_map/ppermute | solution.py:25
  114.1 3.2 %collective-permute-start.16 = (bf16[512,2,128]{2,0,1:T(8,128)(2,1)S(1)}, bf16[512,2,128]{2,0,1:T(8,128)(2,1)S(1)}, u32[]{:S(2)}, u32[]{:S(2)}) collective-permute-start(bf16[512,2,128]{2,0,1:T(8,128)(2,1)S(1)} %collective-permute-done.15), channel_id=1, source_target_pairs={{1,0},{2,1},{3,2},{4,3},{5,4},{6,5},{7,6},{0,7},{9,8},{10,9},{11,1... | collective-permute-start | bytes 786440 | tf_op jit(solution)/shard_map/ppermute | solution.py:27
  117.3 5.0 %collective-permute-done.13 = bf16[512,2,128]{2,0,1:T(8,128)(2,1)} collective-permute-done((bf16[512,2,128]{2,0,1:T(8,128)(2,1)S(1)}, bf16[512,2,128]{2,0,1:T(8,128)(2,1)}, u32[]{:S(2)}, u32[]{:S(2)}) %collective-permute-start.13) | collective-permute-done | bytes 262176 | tf_op jit(solution)/shard_map/ppermute | solution.py:25
  122.4 3.3 %collective-permute-start.17 = (bf16[512,2,128]{2,0,1:T(8,128)(2,1)S(1)}, bf16[512,2,128]{2,0,1:T(8,128)(2,1)S(1)}, u32[]{:S(2)}, u32[]{:S(2)}) collective-permute-start(bf16[512,2,128]{2,0,1:T(8,128)(2,1)S(1)} %collective-permute-done.16), channel_id=1, source_target_pairs={{1,0},{2,1},{3,2},{4,3},{5,4},{6,5},{7,6},{0,7},{9,8},{10,9},{11,1... | collective-permute-start | bytes 786440 | tf_op jit(solution)/shard_map/ppermute | solution.py:27
  125.7 4.5 %collective-permute-done.14 = bf16[512,2,128]{2,0,1:T(8,128)(2,1)} collective-permute-done((bf16[512,2,128]{2,0,1:T(8,128)(2,1)}, bf16[512,2,128]{2,0,1:T(8,128)(2,1)}, u32[]{:S(2)}, u32[]{:S(2)}) %collective-permute-start.14) | collective-permute-done | bytes 262176 | tf_op jit(solution)/shard_map/ppermute | solution.py:25
  130.2 1.7 %bitcast_dynamic-update-slice_fusion.7 = bf16[8,512,2,128]{3,1,2,0:T(8,128)(2,1)} fusion(bf16[512,2,128]{2,0,1:T(8,128)(2,1)} %collective-permute-done.14), kind=kLoop, calls=%fused_computation.98 | loop fusion | bytes 524288
  131.9 1.7 %bitcast_dynamic-update-slice_fusion.6 = bf16[8,512,2,128]{3,1,2,0:T(8,128)(2,1)} fusion(bf16[8,512,2,128]{3,1,2,0:T(8,128)(2,1)} %bitcast_dynamic-update-slice_fusion.7, bf16[512,2,128]{2,0,1:T(8,128)(2,1)} %collective-permute-done.13), kind=kLoop, calls=%fused_computation.97 | loop fusion | bytes 524288
  138.0 3.7 %gather_fusion = bf16[8,512,2,128]{3,1,2,0:T(8,128)(2,1)} fusion(bf16[8,512,2,128]{3,1,2,0:T(8,128)(2,1)} %bitcast_dynamic-update-slice_fusion, s32[1024]{0:T(1024)S(1)} %pad_clamp_fusion), kind=kCustom, calls=%fused_computation | custom fusion | bytes 4194336 | tf_op jit(solution)/shard_map/gather | solution.py:30
  141.7 3.9 %copy.132 = bf16[512,8,2,128]{0,3,2,1:T(8,128)(2,1)} copy(bf16[512,8,2,128]{3,0,2,1:T(8,128)(2,1)} %bitcast.234) | data formatting | bytes 4194304 | tf_op jit(solution)/shard_map/transpose | solution.py:13
  145.6 3.7 %convolution_convert_fusion = bf16[512,512]{1,0:T(8,128)(2,1)} fusion(bf16[512,2048]{0,1:T(8,128)(2,1)} %bitcast.235, bf16[2048,512]{1,0:T(8,128)(2,1)S(1)} %copy-done), kind=kOutput, calls=%fused_computation.3 | convolution fusion | flops 1074003968 | bytes 4718592 | tf_op jit(solution)/shard_map/dot_general | solution.py:188
  (172 shorter events, 38.7 us)
Async XLA Ops:
  0.0 145.6 %copy-start = (bf16[2048,512]{1,0:T(8,128)(2,1)S(1)}, bf16[2048,512]{1,0:T(8,128)(2,1)}, u32[]{:S(2)}) copy-start(bf16[2048,512]{1,0:T(8,128)(2,1)} %param.35) | copy-start | bytes 6291460
  1.1 20.2 %copy-start.3 = (bf16[512,2,128]{2,0,1:T(8,128)(2,1)}, bf16[512,2,128]{2,0,1:T(8,128)(2,1)S(1)}, u32[]{:S(2)}) copy-start(bf16[512,2,128]{2,0,1:T(8,128)(2,1)S(1)} %copy.109) | copy-start | bytes 786436
  2.2 19.1 %copy-start.4 = (bf16[512,2,128]{2,0,1:T(8,128)(2,1)}, bf16[512,2,128]{2,0,1:T(8,128)(2,1)S(1)}, u32[]{:S(2)}) copy-start(bf16[512,2,128]{2,0,1:T(8,128)(2,1)S(1)} %copy.108) | copy-start | bytes 786436
  4.0 16.7 %collective-permute-start = (bf16[3,3,2,128]{3,1,2,0:T(4,128)(2,1)}, bf16[3,3,2,128]{3,1,2,0:T(4,128)(2,1)}, u32[]{:S(2)}, u32[]{:S(2)}) collective-permute-start(bf16[3,3,2,128]{3,1,2,0:T(4,128)(2,1)} %pad_maximum_fusion.3), channel_id=1, source_target_pairs={{0,8},{8,16},{16,24},{24,32},{32,40},{40,48},{48,56},{56,64},{64,7... | collective-permute-start | bytes 13832 | tf_op jit(solution)/shard_map/ppermute | solution.py:41
  8.1 9.0 %copy-start.5 = (f32[128,128]{1,0:T(8,128)}, f32[128,128]{1,0:T(8,128)S(1)}, u32[]{:S(2)}) copy-start(f32[128,128]{1,0:T(8,128)S(1)} %fusion.84) | copy-start | bytes 196612
  18.5 6.1 %copy-start.1 = (f32[8,2,64,64]{3,2,1,0:T(8,128)}, f32[8,2,64,64]{3,2,1,0:T(8,128)S(1)}, u32[]{:S(2)}) copy-start(f32[8,2,64,64]{3,2,1,0:T(8,128)S(1)} %broadcast_in_dim.63) | copy-start | bytes 786436
  20.6 3.6 %copy-start.18 = (f32[8,2,64]{2,1,0:T(2,128)S(1)}, f32[8,2,64]{2,1,0:T(2,128)}, u32[]{:S(2)}) copy-start(f32[8,2,64]{2,1,0:T(2,128)} %copy.105) | copy-start | bytes 12292
  20.6 4.0 %copy-start.12 = (pred[64,64]{1,0:T(8,128)(4,1)S(1)}, pred[64,64]{1,0:T(8,128)(4,1)}, u32[]{:S(2)}) copy-start(pred[64,64]{1,0:T(8,128)(4,1)} %get-tuple-element.130) | copy-start | bytes 12292
  41.1 8.2 %copy-start.2 = (f32[8,2,128,256]{3,2,1,0:T(8,128)S(1)}, f32[8,2,128,256]{3,2,1,0:T(8,128)}, u32[]{:S(2)}) copy-start(f32[8,2,128,256]{3,2,1,0:T(8,128)} %fusion.41) | copy-start | bytes 6291460
  42.7 6.8 %copy-start.20 = (f32[2,128]{1,0:T(2,128)S(1)}, f32[2,128]{1,0:T(2,128)}, u32[]{:S(2)}) copy-start(f32[2,128]{1,0:T(2,128)} %get-tuple-element.113) | copy-start | bytes 3076
  42.7 6.8 %copy-start.21 = (f32[2,128]{1,0:T(2,128)S(1)}, f32[2,128]{1,0:T(2,128)}, u32[]{:S(2)}) copy-start(f32[2,128]{1,0:T(2,128)} %get-tuple-element.114) | copy-start | bytes 3076
  42.7 6.8 %copy-start.22 = (f32[2,128]{1,0:T(2,128)S(1)}, f32[2,128]{1,0:T(2,128)}, u32[]{:S(2)}) copy-start(f32[2,128]{1,0:T(2,128)} %get-tuple-element.115) | copy-start | bytes 3076
  42.7 6.8 %copy-start.23 = (f32[2,128]{1,0:T(2,128)S(1)}, f32[2,128]{1,0:T(2,128)}, u32[]{:S(2)}) copy-start(f32[2,128]{1,0:T(2,128)} %get-tuple-element.116) | copy-start | bytes 3076
  42.7 14.6 %collective-permute-start.2 = (f32[2,128,128]{2,1,0:T(8,128)S(1)}, f32[2,128,128]{2,1,0:T(8,128)S(1)}, u32[]{:S(2)}, u32[]{:S(2)}) collective-permute-start(f32[2,128,128]{2,1,0:T(8,128)S(1)} %get-tuple-element.105), channel_id=1, source_target_pairs={{0,8},{8,16},{16,24},{24,32},{32,40},{40,48},{48,56},{56,64},{64,7... | collective-permute-start | bytes 393224 | tf_op jit(solution)/shard_map/ppermute | solution.py:41
  45.9 6.9 %collective-permute-start.1 = (f32[2,128,128]{2,1,0:T(8,128)S(1)}, f32[2,128,128]{2,1,0:T(8,128)S(1)}, u32[]{:S(2)}, u32[]{:S(2)}) collective-permute-start(f32[2,128,128]{2,1,0:T(8,128)S(1)} %get-tuple-element.106), channel_id=1, source_target_pairs={{0,8},{8,16},{16,24},{24,32},{32,40},{40,48},{48,56},{56,64},{64,7... | collective-permute-start | bytes 393224 | tf_op jit(solution)/shard_map/ppermute | solution.py:41
  53.0 8.7 %collective-permute-start.3 = (f32[2,128,128]{2,1,0:T(8,128)S(1)}, f32[2,128,128]{2,1,0:T(8,128)S(1)}, u32[]{:S(2)}, u32[]{:S(2)}) collective-permute-start(f32[2,128,128]{2,1,0:T(8,128)S(1)} %convolution_add_fusion.5), channel_id=1, source_target_pairs={{0,16},{8,24},{16,32},{24,40},{32,48},{40,56},{48,64},{56,72},{64,... | collective-permute-start | bytes 393224 | tf_op jit(solution)/shard_map/ppermute | solution.py:41
  57.6 8.4 %collective-permute-start.4 = (f32[2,128,128]{2,1,0:T(8,128)S(1)}, f32[2,128,128]{2,1,0:T(8,128)S(1)}, u32[]{:S(2)}, u32[]{:S(2)}) collective-permute-start(f32[2,128,128]{2,1,0:T(8,128)S(1)} %convolution_select_fusion.3), channel_id=1, source_target_pairs={{0,16},{8,24},{16,32},{24,40},{32,48},{40,56},{48,64},{56,72},{64,... | collective-permute-start | bytes 393224 | tf_op jit(solution)/shard_map/ppermute | solution.py:41
  61.9 8.8 %collective-permute-start.5 = (f32[2,128,128]{2,1,0:T(8,128)S(1)}, f32[2,128,128]{2,1,0:T(8,128)S(1)}, u32[]{:S(2)}, u32[]{:S(2)}) collective-permute-start(f32[2,128,128]{2,1,0:T(8,128)S(1)} %convolution_add_fusion.4), channel_id=1, source_target_pairs={{0,32},{8,40},{16,48},{24,56},{32,64},{40,72},{48,80},{56,88},{64,... | collective-permute-start | bytes 393224 | tf_op jit(solution)/shard_map/ppermute | solution.py:41
  66.3 9.2 %collective-permute-start.6 = (f32[2,128,128]{2,1,0:T(8,128)S(1)}, f32[2,128,128]{2,1,0:T(8,128)S(1)}, u32[]{:S(2)}, u32[]{:S(2)}) collective-permute-start(f32[2,128,128]{2,1,0:T(8,128)S(1)} %convolution_select_fusion.2), channel_id=1, source_target_pairs={{0,32},{8,40},{16,48},{24,56},{32,64},{40,72},{48,80},{56,88},{64,... | collective-permute-start | bytes 393224 | tf_op jit(solution)/shard_map/ppermute | solution.py:41
  71.1 8.2 %collective-permute-start.7 = (f32[2,128,128]{2,1,0:T(8,128)S(1)}, f32[2,128,128]{2,1,0:T(8,128)S(1)}, u32[]{:S(2)}, u32[]{:S(2)}) collective-permute-start(f32[2,128,128]{2,1,0:T(8,128)S(1)} %convolution_add_fusion.3), channel_id=1, source_target_pairs={{0,64},{8,72},{16,80},{24,88},{32,96},{40,104},{48,112},{56,120},{... | collective-permute-start | bytes 393224 | tf_op jit(solution)/shard_map/ppermute | solution.py:41
  75.8 5.9 %collective-permute-start.8 = (f32[2,128,128]{2,1,0:T(8,128)S(1)}, f32[2,128,128]{2,1,0:T(8,128)S(1)}, u32[]{:S(2)}, u32[]{:S(2)}) collective-permute-start(f32[2,128,128]{2,1,0:T(8,128)S(1)} %convolution_select_fusion.1), channel_id=1, source_target_pairs={{0,64},{8,72},{16,80},{24,88},{32,96},{40,104},{48,112},{56,120},{... | collective-permute-start | bytes 393224 | tf_op jit(solution)/shard_map/ppermute | solution.py:41
  79.5 2.8 %collective-permute-start.9 = (f32[2,128,128]{2,1,0:T(8,128)S(1)}, f32[2,128,128]{2,1,0:T(8,128)S(1)}, u32[]{:S(2)}, u32[]{:S(2)}) collective-permute-start(f32[2,128,128]{2,1,0:T(8,128)S(1)} %convolution_add_fusion.2), channel_id=1, source_target_pairs={{0,128},{8,136},{16,144},{24,152},{32,160},{40,168},{48,176},{56,1... | collective-permute-start | bytes 393224 | tf_op jit(solution)/shard_map/ppermute | solution.py:41
  82.6 9.8 %copy-start.7 = (bf16[512,2,128]{2,1,0:T(2,128)(2,1)S(1)}, bf16[512,2,128]{2,1,0:T(2,128)(2,1)}, u32[]{:S(2)}) copy-start(bf16[512,2,128]{2,1,0:T(2,128)(2,1)} %param.29) | copy-start | bytes 786436
  82.6 9.7 %copy-start.25 = (f32[128]{0:T(128)S(1)}, f32[128]{0:T(128)}, u32[]{:S(2)}) copy-start(f32[128]{0:T(128)} %param.34) | copy-start | bytes 1540
  82.6 8.8 %collective-permute-start.10 = (f32[2,128,128]{2,1,0:T(8,128)S(1)}, f32[2,128,128]{2,1,0:T(8,128)S(1)}, u32[]{:S(2)}, u32[]{:S(2)}) collective-permute-start(f32[2,128,128]{2,1,0:T(8,128)S(1)} %convolution_add_fusion.1), channel_id=1, source_target_pairs={{0,8},{8,16},{16,24},{24,32},{32,40},{40,48},{48,56},{56,64},{64,7... | collective-permute-start | bytes 393224 | tf_op jit(solution)/shard_map/ppermute | solution.py:41
  92.6 12.5 %collective-permute-start.11 = (bf16[512,2,128]{2,0,1:T(8,128)(2,1)S(1)}, bf16[512,2,128]{2,0,1:T(8,128)(2,1)S(1)}, u32[]{:S(2)}, u32[]{:S(2)}) collective-permute-start(bf16[512,2,128]{2,0,1:T(8,128)(2,1)S(1)} %fusion.28), channel_id=1, source_target_pairs={{0,1},{1,2},{2,3},{3,4},{4,5},{5,6},{6,7},{7,0},{8,9},{9,10},{10,1... | collective-permute-start | bytes 786440 | tf_op jit(solution)/shard_map/ppermute | solution.py:25
  105.1 9.0 %collective-permute-start.12 = (bf16[512,2,128]{2,0,1:T(8,128)(2,1)S(1)}, bf16[512,2,128]{2,0,1:T(8,128)(2,1)S(1)}, u32[]{:S(2)}, u32[]{:S(2)}) collective-permute-start(bf16[512,2,128]{2,0,1:T(8,128)(2,1)S(1)} %collective-permute-done.11), channel_id=1, source_target_pairs={{0,1},{1,2},{2,3},{3,4},{4,5},{5,6},{6,7},{7,0},{8,9},{9,10},{10,1... | collective-permute-start | bytes 786440 | tf_op jit(solution)/shard_map/ppermute | solution.py:25
  105.1 9.0 %collective-permute-start.15 = (bf16[512,2,128]{2,0,1:T(8,128)(2,1)S(1)}, bf16[512,2,128]{2,0,1:T(8,128)(2,1)S(1)}, u32[]{:S(2)}, u32[]{:S(2)}) collective-permute-start(bf16[512,2,128]{2,0,1:T(8,128)(2,1)S(1)} %fusion.28), channel_id=1, source_target_pairs={{1,0},{2,1},{3,2},{4,3},{5,4},{6,5},{7,6},{0,7},{9,8},{10,9},{11,1... | collective-permute-start | bytes 786440 | tf_op jit(solution)/shard_map/ppermute | solution.py:27
  114.1 8.2 %collective-permute-start.13 = (bf16[512,2,128]{2,0,1:T(8,128)(2,1)S(1)}, bf16[512,2,128]{2,0,1:T(8,128)(2,1)}, u32[]{:S(2)}, u32[]{:S(2)}) collective-permute-start(bf16[512,2,128]{2,0,1:T(8,128)(2,1)S(1)} %collective-permute-done.12), channel_id=1, source_target_pairs={{0,1},{1,2},{2,3},{3,4},{4,5},{5,6},{6,7},{7,0},{8,9},{9,10},{10,1... | collective-permute-start | bytes 786440 | tf_op jit(solution)/shard_map/ppermute | solution.py:25
  114.1 8.3 %collective-permute-start.16 = (bf16[512,2,128]{2,0,1:T(8,128)(2,1)S(1)}, bf16[512,2,128]{2,0,1:T(8,128)(2,1)S(1)}, u32[]{:S(2)}, u32[]{:S(2)}) collective-permute-start(bf16[512,2,128]{2,0,1:T(8,128)(2,1)S(1)} %collective-permute-done.15), channel_id=1, source_target_pairs={{1,0},{2,1},{3,2},{4,3},{5,4},{6,5},{7,6},{0,7},{9,8},{10,9},{11,1... | collective-permute-start | bytes 786440 | tf_op jit(solution)/shard_map/ppermute | solution.py:27
  122.3 7.9 %collective-permute-start.14 = (bf16[512,2,128]{2,0,1:T(8,128)(2,1)}, bf16[512,2,128]{2,0,1:T(8,128)(2,1)}, u32[]{:S(2)}, u32[]{:S(2)}) collective-permute-start(bf16[512,2,128]{2,0,1:T(8,128)(2,1)} %collective-permute-done.13), channel_id=1, source_target_pairs={{0,1},{1,2},{2,3},{3,4},{4,5},{5,6},{6,7},{7,0},{8,9},{9,10},{10,1... | collective-permute-start | bytes 786440 | tf_op jit(solution)/shard_map/ppermute | solution.py:25
  122.4 14.9 %collective-permute-start.17 = (bf16[512,2,128]{2,0,1:T(8,128)(2,1)S(1)}, bf16[512,2,128]{2,0,1:T(8,128)(2,1)S(1)}, u32[]{:S(2)}, u32[]{:S(2)}) collective-permute-start(bf16[512,2,128]{2,0,1:T(8,128)(2,1)S(1)} %collective-permute-done.16), channel_id=1, source_target_pairs={{1,0},{2,1},{3,2},{4,3},{5,4},{6,5},{7,6},{0,7},{9,8},{10,9},{11,1... | collective-permute-start | bytes 786440 | tf_op jit(solution)/shard_map/ppermute | solution.py:27
  (12 other events, 33.6 us)
